TPU v7x, 32 devices: a whole 2x2x4 slice. The times are simulated.
32 devices in a mesh: group: 2 (over x), seq: 8 (over z, y), clip: 2 (over core).
Axes of the slice: x: 2, y: 2, z: 4, core: 2. Of those that a mesh axis runs over, the one named last changes fastest.
Arguments:
- latent: float32 [4, 8, 256, 128], P(('group', 'clip'), 'seq'), parts along dimension 0, may hold values from -6 to 6
- context: float32 [4, 8, 256, 128], P(('group', 'clip'), 'seq'), parts along dimension 0, may hold values from -6 to 6
- frozen: int32 [16], P('group'), parts along dimension 0, may hold values 0 or 1
- read_list: int32 [16, 3], P('group'), parts along dimension 0, may hold values from -1 to 6, as said below
- w_embed: bfloat16 [128, 1536], replicated, may hold values from -0.5 to 0.5
- w_qkv: bfloat16 [3, 1536, 1536], P(None, None, 'clip')
- w_attn_out: bfloat16 [1536, 1536], P('clip'), may hold values from -0.45898438 to 0.45898438
- w_head: bfloat16 [1536, 256], replicated, may hold values from -0.15625 to 0.15625
Outputs:
- mirrored: float32 [4, 8, 256, 128], P(('group', 'clip'), 'seq'), parts along dimension 0
There are 2 independent parts, one for each index of `group`. A program takes and returns all parts, laid end to end along the dimension named above; an argument that names none is the same for every part. Nothing has to cross between parts.
Inputs may be any that keep to these rules, and one draw needn't show every extreme that they name: `read_list`: row f lists min(f, 3) distinct earlier frames, the first of them f - 1, and -1 in the remaining entries.
All inputs are finite; a program needn't handle non-finite values.
Results may differ from a plain program's by a relative error of at most 0.015.
Values may be sent and summed in bfloat16 or wider, within the bound.
No kernel may reach another device: no remote copies, remote signals or barrier semaphores. Data moves between devices by JAX's collectives and lax.ppermute only.
A program may use at most 128 MiB of HBM per device.

v0:
```python
import math

import jax
import jax.numpy as jnp
from jax import lax
from jax.sharding import PartitionSpec as P

HD = 128
C = 128
SWEEPS = 2


EPSILON = 1e-05
MASKED_SCORE = -1e30


def passed_along(value, axis, steps):
    count = lax.axis_size(axis)
    initial, last = (max(0, -steps), min(count, count - steps))
    return lax.ppermute(value, axis, [(source, source + steps) for source in range(initial, last)])


def from_partner(block, axis, stride):
    count = lax.axis_size(axis)
    route = []
    for low in range(count):
        high = low | 1 << stride
        if high != low and high < count:
            route += [(low, high), (high, low)]
    return lax.ppermute(block, axis, route)


def normalize(values):
    average = jnp.mean(values, axis=-1, keepdims=True)
    centred = values - average
    spread_sq = jnp.mean(centred * centred, axis=-1, keepdims=True)
    return centred * lax.rsqrt(spread_sq + EPSILON)


def route_states(state_set, read_list, seq_count):
    groups, tokens, channels = state_set.shape
    piece_rows = tokens // seq_count
    link_count = read_list.shape[1]
    pieces = state_set.reshape(groups, seq_count, piece_rows, channels)
    spread = lax.all_to_all(pieces, "seq", split_axis=1, concat_axis=1, tiled=True)
    wanted = jnp.maximum(read_list, 0).reshape(-1)
    chosen = jnp.take(spread, wanted, axis=1).reshape(
        groups, seq_count, link_count, piece_rows, channels
    )
    arrived = lax.all_to_all(chosen, "seq", split_axis=1, concat_axis=3, tiled=True)
    return arrived.reshape(groups, link_count, tokens, channels)


def attend(queries, kv_pair, remote, usable):
    groups, tokens, model_width = queries.shape
    head_count = model_width // HD
    link_count = remote.shape[1]
    joined = jnp.concatenate([kv_pair[:, None], remote], axis=1).reshape(
        groups, (link_count + 1) * tokens, 2 * model_width
    )
    key_rows = joined[:, :, :model_width].reshape(groups, -1, head_count, HD)
    value_rows = joined[:, :, model_width:].reshape(groups, -1, head_count, HD)
    query_rows = queries.reshape(groups, tokens, head_count, HD)
    scores = jnp.einsum(
        "gqhd,gkhd->ghqk", query_rows, key_rows, preferred_element_type=jnp.float32
    ) * (1.0 / math.sqrt(HD))
    allowed = jnp.repeat(jnp.concatenate([jnp.ones((1,), dtype=jnp.bool_), usable]), tokens)
    scores = jnp.where(allowed, scores, MASKED_SCORE)
    weights = jax.nn.softmax(scores, axis=-1).astype(jnp.bfloat16)
    attended = jnp.einsum(
        "ghqk,gkhd->gqhd", weights, value_rows, preferred_element_type=jnp.float32
    )
    return attended.astype(jnp.bfloat16).reshape(groups, tokens, model_width)


def predict(current, read_list, row_links, w_embed, w_head, weight_set, seq_count):
    rounded = current.astype(jnp.bfloat16)
    embedded = jnp.dot(rounded, w_embed, preferred_element_type=jnp.float32)
    normed = normalize(embedded).astype(jnp.bfloat16)
    qkv_set = weight_set[0]
    projected = jnp.einsum(
        "td,jde->jte", normed, qkv_set, preferred_element_type=jnp.float32
    ).astype(jnp.bfloat16)
    projected = projected[:, None]
    queries = projected[0]
    kv_pair = jnp.concatenate([projected[1], projected[2]], axis=-1)
    state_set = rounded[None]
    arrived = route_states(state_set, read_list, seq_count)
    far_embed = jnp.einsum("gltc,cd->gltd", arrived, w_embed, preferred_element_type=jnp.float32)
    far_normed = normalize(far_embed).astype(jnp.bfloat16)
    far_kv = jnp.einsum(
        "gltd,jde->jglte", far_normed, qkv_set[1:], preferred_element_type=jnp.float32
    ).astype(jnp.bfloat16)
    remote = jnp.concatenate([far_kv[0], far_kv[1]], axis=-1)
    attended = attend(queries, kv_pair, remote, row_links >= 0)
    update = jnp.dot(attended[0], weight_set[1], preferred_element_type=jnp.float32)
    residual = embedded + update
    head_in = normalize(residual).astype(jnp.bfloat16)
    return jnp.dot(head_in, w_head, preferred_element_type=jnp.float32)


def per_device(latent, context, frozen, read_list, w_embed, w_qkv, w_attn_out, w_head):
    position = lax.axis_index("seq")
    seq_count = lax.axis_size("seq")
    layout = latent.shape
    latent_rows = latent.reshape(layout[-2], layout[-1])
    context_rows = context.reshape(layout[-2], layout[-1])
    frozen_here = lax.dynamic_index_in_dim(frozen, position, 0, keepdims=False) == 1
    row_links = lax.dynamic_index_in_dim(read_list, position, 0, keepdims=False)
    current = jnp.where(frozen_here, context_rows, latent_rows)
    weight_set = None
    weight_set = (
        lax.all_gather(w_qkv, "clip", axis=2, tiled=True),
        lax.all_gather(w_attn_out, "clip", axis=0, tiled=True),
    )
    for sweep_index in range(SWEEPS):
        predicted = predict(current, read_list, row_links, w_embed, w_head, weight_set, seq_count)
        previous = passed_along(predicted.astype(jnp.bfloat16), "seq", 1).astype(predicted.dtype)
        moved = latent_rows * jnp.exp(jnp.tanh(previous[:, C:])) + previous[:, :C]
        current = jnp.where(frozen_here, context_rows, moved)
    flipped = current[::-1]
    for bit_number in range(seq_count.bit_length() - 1):
        flipped = from_partner(flipped.astype(jnp.bfloat16), "seq", bit_number).astype(
            flipped.dtype
        )
    return flipped.reshape(layout)


def solution(mesh):
    return jax.shard_map(
        per_device,
        mesh=mesh,
        in_specs=(
            P(("group", "clip"), "seq", None, None),
            P(("group", "clip"), "seq", None, None),
            P("group"),
            P("group", None),
            P(),
            P(None, None, "clip"),
            P("clip", None),
            P(),
        ),
        out_specs=P(("group", "clip"), "seq", None, None),
        check_vma=False,
    )
```

profile of v0, /device:TPU:0, one launch (start us, length us, event | category | flops | bytes accessed | tf_op | source)
XLA Modules:
  0.0 223.7 jit_solution(3261248787877495969)
XLA Ops:
  6.6 0.7 all-gather.3.cloned.1.call-update
  7.3 0.6 dynamic_slice.8
  8.6 0.6 select_convert_fusion
  9.2 7.3 %all-to-all-start = ((bf16[1,8,32,128]{3,2,0,1:T(8,128)(2,1)}), bf16[1,8,32,128]{3,2,0,1:T(8,128)(2,1)S(1)}, u32[]{:S(2)}, u32[]{:S(2)}) async-start(bf16[1,8,32,128]{3,2,0,1:T(8,128)(2,1)} %bitcast.6), calls=%async_computation | async-start | bytes 131072 | tf_op jit(solution)/shard_map/all_to_all | solution.py:45
  16.6 0.7 all-gather.5.cloned.1.call-update
  17.7 0.4 fusion.66
  18.3 0.6 reshape.283
  18.9 4.5 %all-to-all-done = bf16[1,8,32,128]{3,2,0,1:T(8,128)(2,1)S(1)} async-done(((bf16[1,8,32,128]{3,2,0,1:T(8,128)(2,1)}), bf16[1,8,32,128]{3,2,0,1:T(8,128)(2,1)S(1)}, u32[]{:S(2)}, u32[]{:S(2)}) %all-to-all-start) | async-done | bytes 65568 | tf_op jit(solution)/shard_map/all_to_all | solution.py:45
  23.4 0.6 gather_fusion
  24.0 0.8 bitcast_select_fusion.1
  24.8 3.4 %all-to-all-start.1 = ((bf16[1,8,3,32,128]{4,3,2,0,1:T(8,128)(2,1)}), bf16[1,8,3,32,128]{4,3,2,0,1:T(8,128)(2,1)S(1)}, u32[]{:S(2)}, u32[]{:S(2)}) async-start(bf16[1,8,3,32,128]{4,3,2,0,1:T(8,128)(2,1)} %bitcast.10), calls=%async_computation.1 | async-start | bytes 393216 | tf_op jit(solution)/shard_map/all_to_all | solution.py:50
  28.5 7.4 %all-to-all-done.1 = bf16[1,8,3,32,128]{4,3,2,0,1:T(8,128)(2,1)S(1)} async-done(((bf16[1,8,3,32,128]{4,3,2,0,1:T(8,128)(2,1)}), bf16[1,8,3,32,128]{4,3,2,0,1:T(8,128)(2,1)S(1)}, u32[]{:S(2)}, u32[]{:S(2)}) %all-to-all-start.1) | async-done | bytes 196640 | tf_op jit(solution)/shard_map/all_to_all | solution.py:50
  35.9 0.8 fusion.67
  36.8 2.1 copy-done.1
  38.9 0.6 multiply_reduce_fusion.1
  39.6 9.2 %fusion.14 = bf16[3,256,1536]{2,1,0:T(8,128)(2,1)S(1)} fusion(bf16[3,1536,1536]{2,1,0:T(8,128)(2,1)} %all-gather.3.cloned.1.call-done, f32[256,1536]{1,0:T(8,128)S(1)} %get-tuple-element.21, f32[256]{0:T(256)S(1)} %add_rsqrt_fusion.5, f32[256]{0:T(256)S(1)} %broadcast_multiply_fusion.5), kind=kOutput, calls=%fused_computation.33 | convolution fusion | flops 3626237952 | bytes 18089984 | tf_op jit(solution)/shard_map/td,jde->jte/dot_general | solution.py:81
  49.0 2.9 %copy-done.2 = f32[3,256,1536]{2,1,0:T(8,128)S(1)} copy-done((f32[3,256,1536]{2,1,0:T(8,128)S(1)}, f32[3,256,1536]{2,1,0:T(8,128)}, u32[]{:S(2)}) %copy-start.2) | copy-done | bytes 4718616
  51.8 10.2 %convert_bitcast_fusion.1 = bf16[2,1,3,256,1536]{4,3,0,2,1:T(8,128)(2,1)S(1)} fusion(bf16[3,1536,1536]{2,1,0:T(8,128)(2,1)} %all-gather.3.cloned.1.call-done, f32[3,256,1536]{2,1,0:T(8,128)S(1)} %copy-done.2, f32[3,256]{1,0:T(4,128)S(1)} %add_rsqrt_fusion.1, f32[3,256]{1,0:T(4,128)S(1)} %broadcast_multiply_fusion.1), kind=kOutput, calls=%fused_computation.28 | convolution fusion | flops 7253655552 | bytes 18880512 | tf_op jit(solution)/shard_map/gltd,jde->jglte/dot_general | solution.py:91
  62.2 0.6 slice_bitcast_fusion.10
  62.8 2.0 maximum_maximum_fusion
  64.8 3.1 %fusion.63 = (bf16[1,1024,1536]{2,1,0:T(8,128)(2,1)}, bf16[1,1024,1536]{2,1,0:T(8,128)(2,1)}) fusion(bf16[1,1024,3072]{2,1,0:T(8,128)(2,1)S(1)} %bitcast.150), kind=kLoop, calls=%fused_computation.120 | loop fusion | bytes 12582912 | tf_op jit(solution)/shard_map/slice | solution.py:61
  67.9 4.6 %copy.36 = bf16[1,1024,1536]{1,2,0:T(8,128)(2,1)} copy(bf16[1,1024,1536]{2,1,0:T(8,128)(2,1)} %get-tuple-element.9) | data formatting | bytes 6291456 | tf_op jit(solution)/shard_map/slice | solution.py:62
  72.5 1.2 copy.37
  73.7 4.8 %copy.57 = bf16[1,1024,1536]{1,2,0:T(8,128)(2,1)} copy(bf16[1,1024,1536]{2,1,0:T(8,128)(2,1)} %get-tuple-element.8) | data formatting | bytes 6291456
  78.5 11.6 %fusion.68 = (f32[12,256]{1,0:T(8,128)}, f32[12,256,1024]{2,1,0:T(8,128)}) fusion(pred[1024]{0:T(1024)(128)(4,1)S(1)} %copy-done.14, bf16[256,12,128]{0,2,1:T(8,128)(2,1)S(1)} %bitcast.160, bf16[1024,12,128]{0,2,1:T(8,128)(2,1)} %bitcast.155), kind=kOutput, calls=%fused_computation.125 | convolution fusion | flops 817890304 | bytes 16528384 | tf_op jit(solution)/shard_map/sub | solution.py:69
  90.1 7.8 %fusion.25 = bf16[12,128,256]{2,1,0:T(8,128)(2,1)S(1)} fusion(bf16[1024,12,128]{0,2,1:T(8,128)(2,1)} %bitcast.152, f32[12,256,1024]{2,1,0:T(8,128)} %get-tuple-element.25, f32[12,256]{1,0:T(8,128)} %get-tuple-element.24), kind=kOutput, calls=%fused_computation.58 | convolution fusion | flops 811991040 | bytes 16527360 | tf_op jit(solution)/shard_map/ghqk,gkhd->gqhd/dot_general | solution.py:70
  97.9 3.8 %fusion.69 = (f32[256]{0:T(256)S(1)}, f32[256,1536]{1,0:T(8,128)S(1)}) fusion(f32[256,1536]{1,0:T(8,128)S(1)} %get-tuple-element.21, bf16[256,1536]{0,1:T(8,128)(2,1)S(1)} %bitcast.163, bf16[1536,1536]{1,0:T(8,128)(2,1)} %all-gather.5.cloned.1.call-done), kind=kOutput, calls=%fused_computation.126 | convolution fusion | flops 1208745728 | bytes 8651776 | tf_op jit(solution)/shard_map/dot_general | solution.py:96
  102.1 0.4 convolution_convert_fusion.3
  102.5 2.9 %collective-permute-start = (bf16[256,256]{1,0:T(8,128)(2,1)S(1)}, bf16[256,256]{1,0:T(8,128)(2,1)S(1)}, u32[]{:S(2)}, u32[]{:S(2)}) collective-permute-start(bf16[256,256]{1,0:T(8,128)(2,1)S(1)} %convolution_convert_fusion.3), channel_id=1, source_target_pairs={{0,2},{2,4},{4,6},{6,8},{8,10},{10,12},{12,14},{1,3},{3,5},{5,7},{... | collective-permute-start | bytes 393224 | tf_op jit(solution)/shard_map/ppermute | solution.py:20
  105.4 3.2 %collective-permute-done = bf16[256,256]{1,0:T(8,128)(2,1)S(1)} collective-permute-done((bf16[256,256]{1,0:T(8,128)(2,1)S(1)}, bf16[256,256]{1,0:T(8,128)(2,1)S(1)}, u32[]{:S(2)}, u32[]{:S(2)}) %collective-permute-start) | collective-permute-done | bytes 131104 | tf_op jit(solution)/shard_map/ppermute | solution.py:20
  108.7 0.7 fusion.50
  109.4 1.3 fusion.70
  110.6 6.5 %all-to-all-start.2 = ((bf16[1,8,32,128]{3,2,0,1:T(8,128)(2,1)}), bf16[1,8,32,128]{3,2,0,1:T(8,128)(2,1)}, u32[]{:S(2)}, u32[]{:S(2)}) async-start(bf16[1,8,32,128]{3,2,0,1:T(8,128)(2,1)} %bitcast.36), calls=%async_computation.2 | async-start | bytes 131072 | tf_op jit(solution)/shard_map/all_to_all | solution.py:45
  117.2 0.3 multiply_reduce_fusion.3
  117.5 9.2 %fusion.15 = bf16[3,256,1536]{2,1,0:T(8,128)(2,1)S(1)} fusion(bf16[3,1536,1536]{2,1,0:T(8,128)(2,1)} %all-gather.3.cloned.1.call-done, f32[256,1536]{1,0:T(8,128)S(1)} %get-tuple-element.29, f32[256]{0:T(256)S(1)} %add_rsqrt_fusion.3, f32[256]{0:T(256)S(1)} %broadcast_multiply_fusion.3), kind=kOutput, calls=%fused_computation.34 | convolution fusion | flops 3626237952 | bytes 18089984 | tf_op jit(solution)/shard_map/td,jde->jte/dot_general | solution.py:81
  126.7 1.3 fusion.64
  128.1 1.2 copy.46
  129.3 1.4 gather_fusion.1
  130.7 0.8 bitcast_select_fusion
  131.4 6.0 %all-to-all-start.3 = ((bf16[1,8,3,32,128]{4,3,2,0,1:T(8,128)(2,1)}), bf16[1,8,3,32,128]{4,3,2,0,1:T(8,128)(2,1)S(1)}, u32[]{:S(2)}, u32[]{:S(2)}) async-start(bf16[1,8,3,32,128]{4,3,2,0,1:T(8,128)(2,1)} %bitcast.40), calls=%async_computation.3 | async-start | bytes 393216 | tf_op jit(solution)/shard_map/all_to_all | solution.py:50
  137.4 2.7 %maximum_bitcast_fusion.1 = bf16[1,1,256,3072]{3,2,1,0:T(8,128)(2,1)} fusion(bf16[1,256,1536]{2,1,0:T(8,128)(2,1)} %get-tuple-element.15, bf16[1,256,1536]{2,1,0:T(8,128)(2,1)} %get-tuple-element.16), kind=kLoop, calls=%fused_computation.48 | loop fusion | flops 3145728 | bytes 3145728 | tf_op jit(solution)/shard_map/broadcast_in_dim | solution.py:58
  140.1 5.1 %all-to-all-done.3 = bf16[1,8,3,32,128]{4,3,2,0,1:T(8,128)(2,1)S(1)} async-done(((bf16[1,8,3,32,128]{4,3,2,0,1:T(8,128)(2,1)}), bf16[1,8,3,32,128]{4,3,2,0,1:T(8,128)(2,1)S(1)}, u32[]{:S(2)}, u32[]{:S(2)}) %all-to-all-start.3) | async-done | bytes 196640 | tf_op jit(solution)/shard_map/all_to_all | solution.py:50
  145.2 0.8 fusion.71
  146.1 0.6 multiply_reduce_fusion
  146.7 10.1 %convert_bitcast_fusion = bf16[2,1,3,256,1536]{4,3,0,2,1:T(8,128)(2,1)S(1)} fusion(bf16[3,1536,1536]{2,1,0:T(8,128)(2,1)} %all-gather.3.cloned.1.call-done, f32[3,256,1536]{2,1,0:T(8,128)S(1)} %get-tuple-element.31, f32[3,256]{1,0:T(4,128)S(1)} %add_rsqrt_fusion, f32[3,256]{1,0:T(4,128)S(1)} %broadcast_multiply_fusion), kind=kOutput, calls=%fused_computation.25 | convolution fusion | flops 7253655552 | bytes 18880512 | tf_op jit(solution)/shard_map/gltd,jde->jglte/dot_general | solution.py:91
  156.9 0.5 slice_bitcast_fusion.8
  157.4 0.8 copy-done.4
  158.3 2.0 maximum_maximum_fusion.1
  160.3 3.1 %fusion.62 = (bf16[1,1024,1536]{2,1,0:T(8,128)(2,1)}, bf16[1,1024,1536]{2,1,0:T(8,128)(2,1)}) fusion(bf16[1,1024,3072]{2,1,0:T(8,128)(2,1)S(1)} %bitcast.151), kind=kLoop, calls=%fused_computation.119 | loop fusion | bytes 12582912 | tf_op jit(solution)/shard_map/slice | solution.py:61
  163.4 4.7 %copy.45 = bf16[1,1024,1536]{1,2,0:T(8,128)(2,1)} copy(bf16[1,1024,1536]{2,1,0:T(8,128)(2,1)} %get-tuple-element.7) | data formatting | bytes 6291456 | tf_op jit(solution)/shard_map/slice | solution.py:62
  168.1 4.8 %copy.59 = bf16[1,1024,1536]{1,2,0:T(8,128)(2,1)} copy(bf16[1,1024,1536]{2,1,0:T(8,128)(2,1)} %get-tuple-element.6) | data formatting | bytes 6291456
  172.8 10.9 %fusion.72 = (f32[12,256]{1,0:T(8,128)S(1)}, f32[12,256,1024]{2,1,0:T(8,128)}) fusion(pred[1024]{0:T(1024)(128)(4,1)S(1)} %copy-done.14, bf16[256,12,128]{0,2,1:T(8,128)(2,1)S(1)} %bitcast.159, bf16[1024,12,128]{0,2,1:T(8,128)(2,1)} %bitcast.154), kind=kOutput, calls=%fused_computation.129 | convolution fusion | flops 817890304 | bytes 16528384 | tf_op jit(solution)/shard_map/sub | solution.py:69
  183.8 7.8 %fusion.24 = bf16[12,128,256]{2,1,0:T(8,128)(2,1)S(1)} fusion(bf16[1024,12,128]{0,2,1:T(8,128)(2,1)} %bitcast.153, f32[12,256,1024]{2,1,0:T(8,128)} %get-tuple-element.33, f32[12,256]{1,0:T(8,128)S(1)} %get-tuple-element.32), kind=kOutput, calls=%fused_computation.57 | convolution fusion | flops 811991040 | bytes 16527360 | tf_op jit(solution)/shard_map/ghqk,gkhd->gqhd/dot_general | solution.py:70
  191.6 3.8 %fusion.73 = (f32[256]{0:T(256)S(1)}, f32[256,1536]{1,0:T(8,128)S(1)}) fusion(f32[256,1536]{1,0:T(8,128)S(1)} %get-tuple-element.29, bf16[256,1536]{0,1:T(8,128)(2,1)S(1)} %bitcast.164, bf16[1536,1536]{1,0:T(8,128)(2,1)} %all-gather.5.cloned.1.call-done), kind=kOutput, calls=%fused_computation.130 | convolution fusion | flops 1208745728 | bytes 8651776 | tf_op jit(solution)/shard_map/dot_general | solution.py:96
  195.8 0.5 convolution_convert_fusion.2
  196.2 2.0 collective-permute-start.1
  198.2 3.2 %collective-permute-done.1 = bf16[256,256]{1,0:T(8,128)(2,1)S(1)} collective-permute-done((bf16[256,256]{1,0:T(8,128)(2,1)S(1)}, bf16[256,256]{1,0:T(8,128)(2,1)S(1)}, u32[]{:S(2)}, u32[]{:S(2)}) %collective-permute-start.1) | collective-permute-done | bytes 131104 | tf_op jit(solution)/shard_map/ppermute | solution.py:20
  201.6 2.5 %collective-permute-start.2 = (bf16[256,128]{1,0:T(8,128)(2,1)S(1)}, bf16[256,128]{1,0:T(8,128)(2,1)S(1)}, u32[]{:S(2)}, u32[]{:S(2)}) collective-permute-start(bf16[256,128]{1,0:T(8,128)(2,1)S(1)} %rev.3), channel_id=1, source_target_pairs={{0,2},{2,0},{4,6},{6,4},{8,10},{10,8},{12,14},{14,12},{1,3},{3,1},... | collective-permute-start | bytes 196616 | tf_op jit(solution)/shard_map/ppermute | solution.py:30
  204.1 2.2 %collective-permute-done.2 = bf16[256,128]{1,0:T(8,128)(2,1)S(1)} collective-permute-done((bf16[256,128]{1,0:T(8,128)(2,1)S(1)}, bf16[256,128]{1,0:T(8,128)(2,1)S(1)}, u32[]{:S(2)}, u32[]{:S(2)}) %collective-permute-start.2) | collective-permute-done | bytes 65568 | tf_op jit(solution)/shard_map/ppermute | solution.py:30
  206.4 2.1 collective-permute-start.3
  208.5 2.5 %collective-permute-done.3 = bf16[256,128]{1,0:T(8,128)(2,1)S(1)} collective-permute-done((bf16[256,128]{1,0:T(8,128)(2,1)S(1)}, bf16[256,128]{1,0:T(8,128)(2,1)S(1)}, u32[]{:S(2)}, u32[]{:S(2)}) %collective-permute-start.3) | collective-permute-done | bytes 65568 | tf_op jit(solution)/shard_map/ppermute | solution.py:30
  211.0 2.3 %collective-permute-start.4 = (bf16[256,128]{1,0:T(8,128)(2,1)S(1)}, bf16[256,128]{1,0:T(8,128)(2,1)S(1)}, u32[]{:S(2)}, u32[]{:S(2)}) collective-permute-start(bf16[256,128]{1,0:T(8,128)(2,1)S(1)} %collective-permute-done.3), channel_id=1, source_target_pairs={{0,8},{8,0},{2,10},{10,2},{4,12},{12,4},{6,14},{14,6},{1,9},{9,1},... | collective-permute-start | bytes 196616 | tf_op jit(solution)/shard_map/ppermute | solution.py:30
  213.3 2.8 %collective-permute-done.4 = bf16[256,128]{1,0:T(8,128)(2,1)S(1)} collective-permute-done((bf16[256,128]{1,0:T(8,128)(2,1)S(1)}, bf16[256,128]{1,0:T(8,128)(2,1)S(1)}, u32[]{:S(2)}, u32[]{:S(2)}) %collective-permute-start.4) | collective-permute-done | bytes 65568 | tf_op jit(solution)/shard_map/ppermute | solution.py:30
  216.2 0.7 bitcast_convert_fusion
  (66 shorter events, 2.3 us)
Async XLA Ops:
  6.5 95.5 %copy-start = (bf16[1536,256]{1,0:T(8,128)(2,1)S(1)}, bf16[1536,256]{1,0:T(8,128)(2,1)}, u32[]{:S(2)}) copy-start(bf16[1536,256]{1,0:T(8,128)(2,1)} %param.17) | copy-start | bytes 2359300
  6.5 0.8 copy-start.15
  6.5 2.0 copy-start.5
  6.5 2.0 copy-start.8
  6.5 10.7 %copy-start.13 = (s32[8,3]{0,1:T(4,128)S(1)}, s32[8,3]{0,1:T(4,128)}, u32[]{:S(2)}) copy-start(s32[8,3]{0,1:T(4,128)} %param.13) | copy-start | bytes 292
  6.5 11.1 %copy-start.3 = (bf16[128,1536]{1,0:T(8,128)(2,1)S(1)}, bf16[128,1536]{1,0:T(8,128)(2,1)}, u32[]{:S(2)}) copy-start(bf16[128,1536]{1,0:T(8,128)(2,1)} %param.14) | copy-start | bytes 1179652
  6.6 33.0 %all-gather.3.cloned.1.call-start = ((), (), s32[]{:S(2)}) async-start(), calls=%async_computation.4 | async-start | bytes 21233664 | tf_op jit(solution)/shard_map/all_gather | solution.py:113
  9.2 14.2 %all-to-all-start = ((bf16[1,8,32,128]{3,2,0,1:T(8,128)(2,1)}), bf16[1,8,32,128]{3,2,0,1:T(8,128)(2,1)S(1)}, u32[]{:S(2)}, u32[]{:S(2)}) async-start(bf16[1,8,32,128]{3,2,0,1:T(8,128)(2,1)} %bitcast.6), calls=%async_computation | async-start | bytes 131072 | tf_op jit(solution)/shard_map/all_to_all | solution.py:45
  16.5 81.4 %all-gather.5.cloned.1.call-start = ((), (), s32[]{:S(2)}) async-start(), calls=%async_computation.5 | async-start | bytes 7077888 | tf_op jit(solution)/shard_map/all_gather | solution.py:114
  24.8 11.1 %all-to-all-start.1 = ((bf16[1,8,3,32,128]{4,3,2,0,1:T(8,128)(2,1)}), bf16[1,8,3,32,128]{4,3,2,0,1:T(8,128)(2,1)S(1)}, u32[]{:S(2)}, u32[]{:S(2)}) async-start(bf16[1,8,3,32,128]{4,3,2,0,1:T(8,128)(2,1)} %bitcast.10), calls=%async_computation.1 | async-start | bytes 393216 | tf_op jit(solution)/shard_map/all_to_all | solution.py:50
  36.8 2.1 copy-start.1
  48.8 3.0 %copy-start.2 = (f32[3,256,1536]{2,1,0:T(8,128)S(1)}, f32[3,256,1536]{2,1,0:T(8,128)}, u32[]{:S(2)}) copy-start(f32[3,256,1536]{2,1,0:T(8,128)} %copy-done.1) | copy-start | bytes 14155780
  73.7 4.8 %copy-start.12 = (bf16[1,256,1536]{1,2,0:T(8,128)(2,1)S(1)}, bf16[1,256,1536]{1,2,0:T(8,128)(2,1)}, u32[]{:S(2)}) copy-start(bf16[1,256,1536]{1,2,0:T(8,128)(2,1)} %copy.37) | copy-start | bytes 2359300
  73.7 4.8 %copy-start.14 = (pred[1024]{0:T(1024)(128)(4,1)S(1)}, pred[1024]{0:T(1024)(128)(4,1)}, u32[]{:S(2)}) copy-start(pred[1024]{0:T(1024)(128)(4,1)} %reshape.283) | copy-start | bytes 3076
  101.7 7.0 %copy-start.6 = (f32[1,1,256,128]{3,2,1,0:T(8,128)S(1)}, f32[1,1,256,128]{3,2,1,0:T(8,128)}, u32[]{:S(2)}) copy-start(f32[1,1,256,128]{3,2,1,0:T(8,128)} %param.10) | copy-start | bytes 393220
  101.7 7.0 %copy-start.9 = (f32[1,1,256,128]{3,2,1,0:T(8,128)S(1)}, f32[1,1,256,128]{3,2,1,0:T(8,128)}, u32[]{:S(2)}) copy-start(f32[1,1,256,128]{3,2,1,0:T(8,128)} %param.11) | copy-start | bytes 393220
  102.5 6.1 %collective-permute-start = (bf16[256,256]{1,0:T(8,128)(2,1)S(1)}, bf16[256,256]{1,0:T(8,128)(2,1)S(1)}, u32[]{:S(2)}, u32[]{:S(2)}) collective-permute-start(bf16[256,256]{1,0:T(8,128)(2,1)S(1)} %convolution_convert_fusion.3), channel_id=1, source_target_pairs={{0,2},{2,4},{4,6},{6,8},{8,10},{10,12},{12,14},{1,3},{3,5},{5,7},{... | collective-permute-start | bytes 393224 | tf_op jit(solution)/shard_map/ppermute | solution.py:20
  110.6 18.6 %all-to-all-start.2 = ((bf16[1,8,32,128]{3,2,0,1:T(8,128)(2,1)}), bf16[1,8,32,128]{3,2,0,1:T(8,128)(2,1)}, u32[]{:S(2)}, u32[]{:S(2)}) async-start(bf16[1,8,32,128]{3,2,0,1:T(8,128)(2,1)} %bitcast.36), calls=%async_computation.2 | async-start | bytes 131072 | tf_op jit(solution)/shard_map/all_to_all | solution.py:45
  131.4 13.8 %all-to-all-start.3 = ((bf16[1,8,3,32,128]{4,3,2,0,1:T(8,128)(2,1)}), bf16[1,8,3,32,128]{4,3,2,0,1:T(8,128)(2,1)S(1)}, u32[]{:S(2)}, u32[]{:S(2)}) async-start(bf16[1,8,3,32,128]{4,3,2,0,1:T(8,128)(2,1)} %bitcast.40), calls=%async_computation.3 | async-start | bytes 393216 | tf_op jit(solution)/shard_map/all_to_all | solution.py:50
  156.8 1.4 copy-start.4
  168.1 4.8 %copy-start.11 = (bf16[1,256,1536]{1,2,0:T(8,128)(2,1)S(1)}, bf16[1,256,1536]{1,2,0:T(8,128)(2,1)}, u32[]{:S(2)}) copy-start(bf16[1,256,1536]{1,2,0:T(8,128)(2,1)} %copy.46) | copy-start | bytes 2359300
  195.4 6.0 %copy-start.7 = (f32[1,1,256,128]{3,2,1,0:T(8,128)S(1)}, f32[1,1,256,128]{3,2,1,0:T(8,128)}, u32[]{:S(2)}) copy-start(f32[1,1,256,128]{3,2,1,0:T(8,128)} %param.10) | copy-start | bytes 393220
  195.4 6.0 %copy-start.10 = (f32[1,1,256,128]{3,2,1,0:T(8,128)S(1)}, f32[1,1,256,128]{3,2,1,0:T(8,128)}, u32[]{:S(2)}) copy-start(f32[1,1,256,128]{3,2,1,0:T(8,128)} %param.11) | copy-start | bytes 393220
  196.2 5.2 %collective-permute-start.1 = (bf16[256,256]{1,0:T(8,128)(2,1)S(1)}, bf16[256,256]{1,0:T(8,128)(2,1)S(1)}, u32[]{:S(2)}, u32[]{:S(2)}) collective-permute-start(bf16[256,256]{1,0:T(8,128)(2,1)S(1)} %convolution_convert_fusion.2), channel_id=1, source_target_pairs={{0,2},{2,4},{4,6},{6,8},{8,10},{10,12},{12,14},{1,3},{3,5},{5,7},{... | collective-permute-start | bytes 393224 | tf_op jit(solution)/shard_map/ppermute | solution.py:20
  201.6 4.8 %collective-permute-start.2 = (bf16[256,128]{1,0:T(8,128)(2,1)S(1)}, bf16[256,128]{1,0:T(8,128)(2,1)S(1)}, u32[]{:S(2)}, u32[]{:S(2)}) collective-permute-start(bf16[256,128]{1,0:T(8,128)(2,1)S(1)} %rev.3), channel_id=1, source_target_pairs={{0,2},{2,0},{4,6},{6,4},{8,10},{10,8},{12,14},{14,12},{1,3},{3,1},... | collective-permute-start | bytes 196616 | tf_op jit(solution)/shard_map/ppermute | solution.py:30
  206.4 4.6 %collective-permute-start.3 = (bf16[256,128]{1,0:T(8,128)(2,1)S(1)}, bf16[256,128]{1,0:T(8,128)(2,1)S(1)}, u32[]{:S(2)}, u32[]{:S(2)}) collective-permute-start(bf16[256,128]{1,0:T(8,128)(2,1)S(1)} %collective-permute-done.2), channel_id=1, source_target_pairs={{0,4},{4,0},{2,6},{6,2},{8,12},{12,8},{10,14},{14,10},{1,5},{5,1},... | collective-permute-start | bytes 196616 | tf_op jit(solution)/shard_map/ppermute | solution.py:30
  211.0 5.2 %collective-permute-start.4 = (bf16[256,128]{1,0:T(8,128)(2,1)S(1)}, bf16[256,128]{1,0:T(8,128)(2,1)S(1)}, u32[]{:S(2)}, u32[]{:S(2)}) collective-permute-start(bf16[256,128]{1,0:T(8,128)(2,1)S(1)} %collective-permute-done.3), channel_id=1, source_target_pairs={{0,8},{8,0},{2,10},{10,2},{4,12},{12,4},{6,14},{14,6},{1,9},{9,1},... | collective-permute-start | bytes 196616 | tf_op jit(solution)/shard_map/ppermute | solution.py:30
Sparse Core Ops, SparseCore 0:
  8.9 29.1 all-gather.2
  39.7 15.5 all-gather.4
where the time goes:
time: 225 us; the launch traced here: 224 us
  matrix products  88.8 us (39%)
  local copies, waits for them, and re-layouts  39.4 us (18%)
  starting transfers between devices  35.2 us (16%)
  waiting for transfers between devices  32.4 us (14%)
  between operations  14.5 us (6%)
  other arithmetic  13.3 us (6%)
    sub x2, matrix products, attend(): weights = jax.nn.softmax(scores, axis=-1).astype(jnp.bfloat16)  22.5 us
    dot_general x2, matrix products, predict(): jnp.einsum('gltd,jde->jglte', far_normed, qkv_set[1:], preferred_element_...  20.3 us
    dot_general x2, matrix products, predict(): jnp.einsum('td,jde->jte', normed, qkv_set, preferred_element_type=jnp.flo...  18.5 us
    dot_general x2, matrix products, attend(): jnp.einsum('ghqk,gkhd->gqhd', weights, value_rows, preferred_element_type...  15.6 us
    unnamed x34, local copies, waits for them, and re-layouts  15.4 us
    all_to_all x2, starting transfers between devices, route_states(): lax.all_to_all(pieces, 'seq', split_axis=1, concat_axis=1, tiled=True)  13.9 us
    all_to_all x2, waiting for transfers between devices, route_states(): lax.all_to_all(chosen, 'seq', split_axis=1, concat_axis=3, tiled=True)  12.5 us
    all_to_all x2, starting transfers between devices, route_states(): lax.all_to_all(chosen, 'seq', split_axis=1, concat_axis=3, tiled=True)  9.4 us
  transfers between devices with their start and end apart: 11, of which 8 were waited for; matrix products, arithmetic and copies ran while one was open for 34% of the time, Pallas kernels for 0%

commit v1 on v0

v1 whole, which is shorter than its diff:
```python
import functools
import math

import jax
import jax.numpy as jnp
from jax import lax
from jax.experimental import pallas as pl
from jax.experimental.pallas import tpu as pltpu
from jax.sharding import PartitionSpec as P

HD = 128
EPSILON = 1e-05
F32 = jnp.float32
BF16 = jnp.bfloat16


def split_bf16(value, pieces):
    out = []
    for _ in range(pieces):
        piece = value.astype(BF16)
        out.append(piece)
        value = value - piece.astype(F32)
    return out


def fold_kernel(embed_ref, qkv_ref, folded_ref, gram_ref, centred_ref):
    channels, width = embed_ref.shape

    @pl.when(pl.program_id(0) == 0)
    def _():
        rows = embed_ref[...].astype(F32)
        centred = rows - jnp.mean(rows, axis=1, keepdims=True)
        high, low = split_bf16(centred, 2)
        centred_ref[:channels] = high
        centred_ref[channels:] = low
        gram = lax.dot_general(
            centred, centred, (((1,), (1,)), ((), ())),
            precision=lax.Precision.HIGHEST, preferred_element_type=F32,
        ) * (1.0 / width)
        for index, piece in enumerate(split_bf16(gram, 3)):
            gram_ref[:, index * channels:(index + 1) * channels] = piece

    both = centred_ref[...]
    maps = []
    for index in range(3):
        product = jnp.dot(both, qkv_ref[index], preferred_element_type=F32)
        maps.append(product[:channels] + product[channels:])
    scale = math.log2(math.e) / math.sqrt(HD)
    heads = qkv_ref.shape[2] // HD
    folded_ref[0, channels:] = jnp.zeros((heads * HD, heads * HD), BF16)
    for head in range(heads):
        cols = slice(head * HD, (head + 1) * HD)
        score_map = lax.dot_general(
            maps[0][:, cols], maps[1][:, cols], (((1,), (1,)), ((), ())),
            precision=lax.Precision.HIGHEST, preferred_element_type=F32,
        ) * scale
        folded_ref[0, :channels, cols] = score_map.astype(BF16)
        folded_ref[0, channels + head * HD:channels + (head + 1) * HD, cols] = (
            maps[2][:, cols].astype(BF16)
        )


def fold_weights(w_embed, w_qkv):
    channels, width = w_embed.shape
    cols = w_qkv.shape[2]
    wide = 2 * HD
    pairs = cols // wide
    return pl.pallas_call(
        fold_kernel,
        grid=(pairs,),
        in_specs=[
            pl.BlockSpec((channels, width), lambda i: (0, 0)),
            pl.BlockSpec((3, width, wide), lambda i: (0, 0, i)),
        ],
        out_specs=[
            pl.BlockSpec((1, channels + wide, wide), lambda i: (i, 0, 0)),
            pl.BlockSpec((channels, 3 * channels), lambda i: (0, 0)),
        ],
        out_shape=[
            jax.ShapeDtypeStruct((pairs, channels + wide, wide), BF16),
            jax.ShapeDtypeStruct((channels, 3 * channels), BF16),
        ],
        scratch_shapes=[pltpu.VMEM((2 * channels, width), BF16)],
        cost_estimate=pl.CostEstimate(
            flops=4 * channels * width * 3 * cols, bytes_accessed=6 * width * cols, transcendentals=0
        ),
        name="fold",
    )(w_embed, w_qkv)


def flow_kernel(parts, place_ref, frozen_ref, read_ref, near_ref, far_ref, gram_ref, embed_hbm, head_hbm, *rest):
    folded_hbm, out_hbm = rest[:parts], rest[parts:2 * parts]
    (result_ref, raw, turned, valued, query_raw, query, keys, values, mapped, attended,
     folded, w_embed, w_out, w_head, sems) = rest[2 * parts:]
    half, tokens, channels = near_ref.shape
    frames = 2 * half
    links = read_ref.shape[1]
    slots = links + 1
    pairs_here = folded_hbm[0].shape[0]
    rows_here = out_hbm[0].shape[0]
    place = place_ref[0]

    loads = [
        pltpu.make_async_copy(embed_hbm, w_embed, sems.at[0]),
        pltpu.make_async_copy(head_hbm, w_head, sems.at[1]),
    ]
    folded_loads = []
    for part in range(parts):
        folded_loads.append(pltpu.make_async_copy(
            folded_hbm[part], folded.at[part * pairs_here:(part + 1) * pairs_here], sems.at[2 + part]))
        loads.append(pltpu.make_async_copy(
            out_hbm[part], w_out.at[part * rows_here:(part + 1) * rows_here], sems.at[2 + parts + part]))
    for load in folded_loads + loads:
        load.start()

    def slot_of(frame):
        shift = lax.rem(place // 2 - frame // 2 + half, half)
        return jnp.where(lax.rem(place + frame, 2) == 0, shift, half + shift)

    def ingest(slot, rounded):
        wide = rounded.astype(F32)
        spread = jnp.dot(rounded, gram_ref[...], preferred_element_type=F32)
        spread = spread[:, :channels] + spread[:, channels:2 * channels] + spread[:, 2 * channels:]
        variance = jnp.maximum(jnp.sum(spread * wide, axis=1, keepdims=True), 0.0)
        scaled = (wide * lax.rsqrt(variance + EPSILON)).astype(BF16)
        raw[slot] = rounded
        turned[slot] = scaled.T
        valued[slot, :, :channels] = scaled
        valued[slot, :, channels:] = jnp.ones((tokens, channels), BF16)

    def ingest_step(index, carry):
        ingest(index, near_ref[index])
        ingest(half + index, far_ref[index])
        return carry

    lax.fori_loop(0, half, ingest_step, 0)
    for load in folded_loads + loads:
        load.wait()

    target = frames - 1 - place
    last = target - 1
    last_safe = jnp.maximum(last, 0)
    run_all = jnp.logical_and(target > 0, frozen_ref[target] == 0)

    def flip():
        rows = lax.broadcasted_iota(jnp.int32, (tokens, tokens), 0)
        cols = lax.broadcasted_iota(jnp.int32, (tokens, tokens), 1)
        return jnp.where(rows + cols == tokens - 1, 1.0, 0.0).astype(BF16)

    def source_of(index):
        return jnp.where(index == 0, last_safe, read_ref[last_safe, jnp.maximum(index - 1, 0)])

    def is_run(index):
        frame = source_of(index)
        return jnp.logical_and(frame > 0, frozen_ref[jnp.maximum(frame, 0)] == 0)

    def attend():
        def head_pair(pair, carry):
            contexts = []
            for side in range(2):
                mapped_head = mapped[pair, :, side * HD:(side + 1) * HD]
                scores = jnp.dot(mapped_head, keys[...], preferred_element_type=F32)
                top = jnp.max(scores, axis=1, keepdims=True)
                weights = jnp.exp2(scores - top).astype(BF16)
                total = jnp.dot(weights, values[...], preferred_element_type=F32)
                contexts.append((total[:, :channels] / total[:, channels:]).astype(BF16))
            both = jnp.concatenate(contexts, axis=1)
            attended[:, pl.ds(pl.multiple_of(pair * 2 * HD, 2 * HD), 2 * HD)] = jnp.dot(
                both, folded[pair, channels:], preferred_element_type=F32
            ).astype(BF16)
            return carry

        lax.fori_loop(0, folded.shape[0], head_pair, 0)

    def evaluate():
        def map_pair(pair, carry):
            mapped[pair] = jnp.dot(
                query[...], folded[pair, :channels], preferred_element_type=F32
            ).astype(BF16)
            return carry

        lax.fori_loop(0, folded.shape[0], map_pair, 0)
        attend()
        residual = jnp.dot(query_raw[...], w_embed[...], preferred_element_type=F32) + jnp.dot(
            attended[...], w_out[...], preferred_element_type=F32
        )
        centred = residual - jnp.mean(residual, axis=1, keepdims=True)
        spread_sq = jnp.mean(centred * centred, axis=1, keepdims=True)
        head_in = (centred * lax.rsqrt(spread_sq + EPSILON)).astype(BF16)
        return jnp.dot(head_in, w_head[...], preferred_element_type=F32)

    def moved(held, predicted):
        return held * jnp.exp(jnp.tanh(predicted[:, channels:])) + predicted[:, :channels]

    def place_key(index, slot, usable):
        keys[:, index * tokens:(index + 1) * tokens] = turned[slot]
        block = valued[slot]
        values[index * tokens:(index + 1) * tokens] = jnp.where(usable, block, jnp.zeros_like(block))

    def round_step(step, carry):
        final = step == slots

        @pl.when(jnp.logical_and(run_all, jnp.logical_or(final, is_run(jnp.minimum(step, slots - 1)))))
        def _():
            frame = jnp.where(final, last_safe, source_of(jnp.minimum(step, slots - 1)) - 1)
            frame = jnp.maximum(frame, 0)
            own = jnp.where(jnp.logical_and(final, is_run(0)), frames, slot_of(frame))
            query_raw[...] = raw[own]
            query[...] = valued[own, :, :channels]
            place_key(0, own, True)
            for link in range(links):
                source = read_ref[frame, link]
                usable = source >= 0
                held = slot_of(jnp.maximum(source, 0))
                held = jnp.where(jnp.logical_and(final, is_run(link + 1)), frames + link + 1, held)
                place_key(link + 1, jnp.where(usable, held, own), usable)

            @pl.when(final)
            def _():
                mirror = flip()
                query_raw[...] = jnp.dot(mirror, query_raw[...], preferred_element_type=F32).astype(BF16)
                query[...] = jnp.dot(mirror, query[...], preferred_element_type=F32).astype(BF16)

            predicted = evaluate()

            @pl.when(jnp.logical_not(final))
            def _():
                base = raw[slot_of(frame + 1)].astype(F32)
                ingest(frames + step, moved(base, predicted).astype(BF16))

            @pl.when(final)
            def _():
                base = jnp.dot(flip(), raw[slot_of(target)], preferred_element_type=F32)
                result_ref[...] = moved(base, predicted)

        return carry

    lax.fori_loop(0, slots + 1, round_step, 0)

    @pl.when(jnp.logical_not(run_all))
    def _():
        result_ref[...] = jnp.dot(flip(), raw[slot_of(target)], preferred_element_type=F32)


def run_flow(place, frozen, read_list, near, far, gram, w_embed, w_head, folded, outs):
    half, tokens, channels = near.shape
    frames = 2 * half
    parts = len(folded)
    slots = read_list.shape[1] + 1
    width = w_embed.shape[1]
    pairs = sum(block.shape[0] for block in folded)
    hidden = sum(block.shape[0] for block in outs)
    vmem = pl.BlockSpec(memory_space=pltpu.VMEM)
    smem = pl.BlockSpec(memory_space=pltpu.SMEM)
    anywhere = pl.BlockSpec(memory_space=pl.ANY)
    held = frames + slots
    return pl.pallas_call(
        functools.partial(flow_kernel, parts),
        in_specs=[smem, smem, smem, vmem, vmem, vmem, anywhere, anywhere] + [anywhere] * (2 * parts),
        out_specs=vmem,
        out_shape=jax.ShapeDtypeStruct((tokens, channels), F32),
        scratch_shapes=[
            pltpu.VMEM((held, tokens, channels), BF16),
            pltpu.VMEM((held, channels, tokens), BF16),
            pltpu.VMEM((held, tokens, 2 * channels), BF16),
            pltpu.VMEM((tokens, channels), BF16),
            pltpu.VMEM((tokens, channels), BF16),
            pltpu.VMEM((channels, slots * tokens), BF16),
            pltpu.VMEM((slots * tokens, 2 * channels), BF16),
            pltpu.VMEM((pairs, tokens, 2 * HD), BF16),
            pltpu.VMEM((tokens, hidden), BF16),
            pltpu.VMEM((pairs,) + folded[0].shape[1:], BF16),
            pltpu.VMEM(w_embed.shape, BF16),
            pltpu.VMEM((hidden, width), BF16),
            pltpu.VMEM(w_head.shape, BF16),
            pltpu.SemaphoreType.DMA((2 + 2 * parts,)),
        ],
        compiler_params=pltpu.CompilerParams(vmem_limit_bytes=56 * 1024 * 1024),
        name="flow",
    )(place, frozen, read_list, near, far, gram, w_embed, w_head, *folded, *outs)


def from_behind(value, axis, shift):
    count = lax.axis_size(axis)
    return lax.ppermute(value, axis, [(source, (source + shift) % count) for source in range(count)])


def per_device(latent, context, frozen, read_list, w_embed, w_qkv, w_attn_out, w_head):
    position = lax.axis_index("seq")
    seq_count = lax.axis_size("seq")
    clip_count = lax.axis_size("clip")
    layout = latent.shape
    frozen_here = lax.dynamic_index_in_dim(frozen, position, 0, keepdims=False) == 1
    held = jnp.where(frozen_here, context, latent).astype(BF16).reshape(layout[-2], layout[-1])
    shifted = [held] + [from_behind(held, "seq", 2 * step) for step in range(1, seq_count // 2)]
    near = jnp.stack(shifted)
    far = lax.ppermute(near, "seq", [(source, source ^ 1) for source in range(seq_count)])
    outs = [w_attn_out] + [from_behind(w_attn_out, "clip", step) for step in range(1, clip_count)]
    folded, gram = fold_weights(w_embed, w_qkv)
    folded = [folded] + [from_behind(folded, "clip", step) for step in range(1, clip_count)]
    result = run_flow(
        position.reshape(1).astype(jnp.int32), frozen, read_list, near, far, gram, w_embed, w_head, folded, outs
    )
    return result.reshape(layout)


def solution(mesh):
    return jax.shard_map(
        per_device,
        mesh=mesh,
        in_specs=(
            P(("group", "clip"), "seq", None, None),
            P(("group", "clip"), "seq", None, None),
            P("group"),
            P("group", None),
            P(),
            P(None, None, "clip"),
            P("clip", None),
            P(),
        ),
        out_specs=P(("group", "clip"), "seq", None, None),
        check_vma=False,
    )
```

time: 225 us -> 77 us (0.34)
  matrix products: 88.8 us -> 0 us
  Pallas kernels: 0 us -> 57.2 us
  local copies, waits for them, and re-layouts: 39.4 us -> 3.57 us
  starting transfers between devices: 35.2 us -> 7.74 us
  waiting for transfers between devices: 32.4 us -> 6.52 us
  between operations: 14.5 us -> 0.77 us
  other arithmetic: 13.3 us -> 0.99 us
    dot_general x14 -> x0, matrix products: 66.3 us -> none  [the longest x2 20.3 us: predict(): jnp.einsum('gltd,jde->jglte', far_normed, qkv_set[1:], preferred_element_...]
    pallas_call x0 -> x2, Pallas kernels: none -> 57.2 us  [the longest x1 49.9 us: run_flow(): pl.pallas_call(functools.partial(flow_kernel, parts), in_specs=[smem, sme...]
    all_to_all x4 -> x0, starting transfers between devices: 23.3 us -> none  [the longest x2 13.9 us: route_states(): lax.all_to_all(pieces, 'seq', split_axis=1, concat_axis=1, tiled=True)]
    sub x2 -> x0, matrix products: 22.5 us -> none  [attend(): weights = jax.nn.softmax(scores, axis=-1).astype(jnp.bfloat16)]
    slice x8 -> x0, local copies, waits for them, and re-layouts: 19.4 us -> none  [the longest x2 9.33 us: attend(): value_rows = joined[:, :, model_width:].reshape(groups, -1, head_count, HD)]
    all_to_all x4 -> x0, waiting for transfers between devices: 17.1 us -> none  [the longest x2 12.5 us: route_states(): lax.all_to_all(chosen, 'seq', split_axis=1, concat_axis=3, tiled=True)]
    unnamed x34 -> x15, local copies, waits for them, and re-layouts: 15.4 us -> 2.33 us
    ppermute x5 -> x6, waiting for transfers between devices: 13.9 us -> 6.52 us  [the longest x1 6.51 us: per_device(): lax.ppermute(near, 'seq', [(source, source ^ 1) for source in range(seq_c...]
  transfers between devices with their start and end apart: 11 -> 6, of which waited for: 8 -> 1; matrix products, arithmetic and copies ran while one was open for 34% -> 4% of each run, Pallas kernels for 0% -> 10%
where the time goes in v1:
time: 77 us; the launch traced here: 76.8 us
  Pallas kernels  57.2 us (74%)
  starting transfers between devices  7.74 us (10%)
  waiting for transfers between devices  6.52 us (8%)
  local copies, waits for them, and re-layouts  3.57 us (5%)
  other arithmetic  0.99 us (1%)
  between operations  0.77 us (1%)
    pallas_call x1, Pallas kernels, run_flow(): pl.pallas_call(functools.partial(flow_kernel, parts), in_specs=[smem, sme...  49.9 us
    pallas_call x1, Pallas kernels, fold_weights(): pl.pallas_call(fold_kernel, grid=(pairs,), in_specs=[pl.BlockSpec((channe...  7.35 us
    ppermute x1, waiting for transfers between devices, per_device(): lax.ppermute(near, 'seq', [(source, source ^ 1) for source in range(seq_c...  6.51 us
    ppermute x5, starting transfers between devices, from_behind(): lax.ppermute(value, axis, [(source, (source + shift) % count) for source...  6.15 us
    unnamed x15, local copies, waits for them, and re-layouts  2.33 us
    ppermute x1, starting transfers between devices, per_device(): lax.ppermute(near, 'seq', [(source, source ^ 1) for source in range(seq_c...  1.59 us
  transfers between devices with their start and end apart: 6, of which 1 were waited for; matrix products, arithmetic and copies ran while one was open for 4% of the time, Pallas kernels for 10%

profile of v1, /device:TPU:0, one launch (start us, length us, event | category | flops | bytes accessed | tf_op | source)
XLA Modules:
  0.0 76.8 jit_solution(4299638968802760953)
XLA Ops:
  0.0 0.5 collective-permute-start.5
  0.5 1.2 %dynamic_slice.4 = s32[1]{0:T(128)} dynamic-slice(s32[8]{0:T(128)} %frozen_ref.1, s32[]{:T(128)S(6)} %select_n.12), dynamic_slice_sizes={1} | dynamic-slice | bytes 12 | tf_op jit(solution)/shard_map/jit(dynamic_index_in_dim)/dynamic_slice | solution.py:293
  2.4 0.9 %fusion.1 = bf16[256,128]{1,0:T(8,128)(2,1)S(1)} fusion(f32[1,1,256,128]{3,2,1,0:T(8,128)} %param.9, f32[1,1,256,128]{3,2,1,0:T(8,128)} %param.8, pred[]{:T(512)} %bitcast.1), kind=kLoop, calls=%fused_computation.3 | loop fusion | flops 32768 | bytes 327681 | tf_op jit(solution)/shard_map/reshape | solution.py:294
  3.3 0.0 copy-start.3
  3.3 0.0 copy-start.4
  3.3 0.0 copy-start.6
  3.4 4.6 %collective-permute-start.2 = (bf16[256,128]{1,0:T(8,128)(2,1)S(1)}, bf16[256,128]{1,0:T(8,128)(2,1)S(1)}, u32[]{:S(2)}, u32[]{:S(2)}) collective-permute-start(bf16[256,128]{1,0:T(8,128)(2,1)S(1)} %fusion.1), channel_id=1, source_target_pairs={{0,12},{2,14},{4,0},{6,2},{8,4},{10,6},{12,8},{14,10},{1,13},{3,15... | collective-permute-start | bytes 196616 | tf_op jit(solution)/shard_map/ppermute | solution.py:285
  8.0 0.0 collective-permute-start.1
  8.0 1.0 %collective-permute-start = (bf16[256,128]{1,0:T(8,128)(2,1)S(1)}, bf16[256,128]{1,0:T(8,128)(2,1)S(1)}, u32[]{:S(2)}, u32[]{:S(2)}) collective-permute-start(bf16[256,128]{1,0:T(8,128)(2,1)S(1)} %fusion.1), channel_id=1, source_target_pairs={{0,4},{2,6},{4,8},{6,10},{8,12},{10,14},{12,0},{14,2},{1,5},{3,7},... | collective-permute-start | bytes 196616 | tf_op jit(solution)/shard_map/ppermute | solution.py:285
  9.0 7.4 %fold.1 = (bf16[3,384,256]{2,1,0:T(8,128)(2,1)}, bf16[128,384]{1,0:T(8,128)(2,1)}) custom-call(bf16[128,1536]{1,0:T(8,128)(2,1)} %embed_hbm.1, bf16[3,1536,768]{2,1,0:T(8,128)(2,1)} %qkv_ref.1), custom_call_target="tpu_custom_call" | custom-call | flops 1811939328 | bytes 7077888 | tf_op jit(solution)/shard_map/fold/pallas_call | solution.py:68
  16.4 0.0 collective-permute-start.4
  16.4 0.0 copy-done.3
  16.4 0.0 copy-done.4
  16.4 0.0 collective-permute-done.2
  16.4 0.0 collective-permute-done.1
  16.4 0.0 collective-permute-done
  16.5 0.0 copy-start.1
  16.5 1.6 %collective-permute-start.3 = (bf16[4,256,128]{2,1,0:T(8,128)(2,1)S(1)}, bf16[4,256,128]{2,1,0:T(8,128)(2,1)S(1)}, u32[]{:S(2)}, u32[]{:S(2)}) collective-permute-start(bf16[4,256,128]{2,1,0:T(8,128)(2,1)S(1)} %pad_maximum_fusion.near_ref), channel_id=1, source_target_pairs={{0,2},{2,0},{4,6},{6,4},{8,10},{10,8},{12,14},{14,12},{1,3},{3,1},... | collective-permute-start | bytes 786440 | tf_op jit(solution)/shard_map/ppermute | solution.py:297
  18.1 0.0 copy-done.6
  18.1 0.7 copy.9.read_ref
  18.8 6.5 %collective-permute-done.3.far_ref = bf16[4,256,128]{2,1,0:T(8,128)(2,1)S(1)} collective-permute-done((bf16[4,256,128]{2,1,0:T(8,128)(2,1)S(1)}, bf16[4,256,128]{2,1,0:T(8,128)(2,1)S(1)}, u32[]{:S(2)}, u32[]{:S(2)}) %collective-permute-start.3) | collective-permute-done | bytes 262176 | tf_op jit(solution)/shard_map/ppermute | solution.py:297
  25.3 0.0 copy-start.5
  25.3 0.0 collective-permute-done.4.rest_1_
  25.3 0.0 copy-start.2
  25.3 0.0 collective-permute-done.5.rest_3_
  25.3 0.0 copy-start
  25.3 0.0 copy-done.1
  25.3 0.7 copy-done.5
  26.0 0.2 copy-done.2
  26.2 0.8 %copy-done = bf16[768,1536]{1,0:T(8,128)(2,1)} copy-done((bf16[768,1536]{1,0:T(8,128)(2,1)}, bf16[768,1536]{1,0:T(8,128)(2,1)S(1)}, u32[]{:S(2)}) %copy-start) | copy-done | bytes 2359320
  26.9 49.9 %flow.1 = f32[256,128]{1,0:T(8,128)} custom-call(s32[1]{0:T(128)} %bitcast.place_ref, s32[8]{0:T(128)} %frozen_ref.1, s32[8,3]{1,0:T(8,128)} %copy.9.read_ref, bf16[4,256,128]{2,1,0:T(8,128)(2,1)} %copy-done.1, bf16[4,256,128]{2,1,0:T(8,128)(2,1)} %copy-done.5, bf16[128,384]{1,0:T(8,128)(2,1)} %get-tuple-element.7.gram_ref, bf16[128,1536]{1,0:T(8,128)(2,1)} %embed_hbm.1, ...), custom_call_target="tpu_custom_call" | custom-call | tf_op jit(solution)/shard_map/flow/pallas_call | solution.py:257
  (2 shorter events, 0.1 us)
Async XLA Ops:
  0.0 25.3 %collective-permute-start.5 = (bf16[768,1536]{1,0:T(8,128)(2,1)}, bf16[768,1536]{1,0:T(8,128)(2,1)S(1)}, u32[]{:S(2)}, u32[]{:S(2)}) collective-permute-start(bf16[768,1536]{1,0:T(8,128)(2,1)} %rest_2_.1), channel_id=1, source_target_pairs={{0,1},{1,0},{2,3},{3,2},{4,5},{5,4},{6,7},{7,6},{8,9},{9,8},{10,11... | collective-permute-start | bytes 7077896 | tf_op jit(solution)/shard_map/ppermute | solution.py:285
  3.3 13.0 %copy-start.3 = (f32[1,1,256,128]{3,2,1,0:T(8,128)S(1)}, f32[1,1,256,128]{3,2,1,0:T(8,128)}, u32[]{:S(2)}) copy-start(f32[1,1,256,128]{3,2,1,0:T(8,128)} %param.9) | copy-start | bytes 393220
  3.3 13.0 %copy-start.4 = (f32[1,1,256,128]{3,2,1,0:T(8,128)S(1)}, f32[1,1,256,128]{3,2,1,0:T(8,128)}, u32[]{:S(2)}) copy-start(f32[1,1,256,128]{3,2,1,0:T(8,128)} %param.8) | copy-start | bytes 393220
  3.3 14.7 %copy-start.6 = (s32[8,3]{0,1:T(4,128)S(1)}, s32[8,3]{0,1:T(4,128)}, u32[]{:S(2)}) copy-start(s32[8,3]{0,1:T(4,128)} %param.11) | copy-start | bytes 292
  3.4 13.1 %collective-permute-start.2 = (bf16[256,128]{1,0:T(8,128)(2,1)S(1)}, bf16[256,128]{1,0:T(8,128)(2,1)S(1)}, u32[]{:S(2)}, u32[]{:S(2)}) collective-permute-start(bf16[256,128]{1,0:T(8,128)(2,1)S(1)} %fusion.1), channel_id=1, source_target_pairs={{0,12},{2,14},{4,0},{6,2},{8,4},{10,6},{12,8},{14,10},{1,13},{3,15... | collective-permute-start | bytes 196616 | tf_op jit(solution)/shard_map/ppermute | solution.py:285
  8.0 8.4 %collective-permute-start.1 = (bf16[256,128]{1,0:T(8,128)(2,1)S(1)}, bf16[256,128]{1,0:T(8,128)(2,1)S(1)}, u32[]{:S(2)}, u32[]{:S(2)}) collective-permute-start(bf16[256,128]{1,0:T(8,128)(2,1)S(1)} %fusion.1), channel_id=1, source_target_pairs={{0,8},{2,10},{4,12},{6,14},{8,0},{10,2},{12,4},{14,6},{1,9},{3,11}... | collective-permute-start | bytes 196616 | tf_op jit(solution)/shard_map/ppermute | solution.py:285
  8.0 8.4 %collective-permute-start = (bf16[256,128]{1,0:T(8,128)(2,1)S(1)}, bf16[256,128]{1,0:T(8,128)(2,1)S(1)}, u32[]{:S(2)}, u32[]{:S(2)}) collective-permute-start(bf16[256,128]{1,0:T(8,128)(2,1)S(1)} %fusion.1), channel_id=1, source_target_pairs={{0,4},{2,6},{4,8},{6,10},{8,12},{10,14},{12,0},{14,2},{1,5},{3,7},... | collective-permute-start | bytes 196616 | tf_op jit(solution)/shard_map/ppermute | solution.py:285
  16.4 8.9 %collective-permute-start.4 = (bf16[3,384,256]{2,1,0:T(8,128)(2,1)}, bf16[3,384,256]{2,1,0:T(8,128)(2,1)S(1)}, u32[]{:S(2)}, u32[]{:S(2)}) collective-permute-start(bf16[3,384,256]{2,1,0:T(8,128)(2,1)} %get-tuple-element.8.rest_0_), channel_id=1, source_target_pairs={{0,1},{1,0},{2,3},{3,2},{4,5},{5,4},{6,7},{7,6},{8,9},{9,8},{10,11... | collective-permute-start | bytes 1769480 | tf_op jit(solution)/shard_map/ppermute | solution.py:285
  16.5 8.8 %copy-start.1 = (bf16[4,256,128]{2,1,0:T(8,128)(2,1)}, bf16[4,256,128]{2,1,0:T(8,128)(2,1)S(1)}, u32[]{:S(2)}) copy-start(bf16[4,256,128]{2,1,0:T(8,128)(2,1)S(1)} %pad_maximum_fusion.near_ref) | copy-start | bytes 786436
  16.5 8.8 %collective-permute-start.3 = (bf16[4,256,128]{2,1,0:T(8,128)(2,1)S(1)}, bf16[4,256,128]{2,1,0:T(8,128)(2,1)S(1)}, u32[]{:S(2)}, u32[]{:S(2)}) collective-permute-start(bf16[4,256,128]{2,1,0:T(8,128)(2,1)S(1)} %pad_maximum_fusion.near_ref), channel_id=1, source_target_pairs={{0,2},{2,0},{4,6},{6,4},{8,10},{10,8},{12,14},{14,12},{1,3},{3,1},... | collective-permute-start | bytes 786440 | tf_op jit(solution)/shard_map/ppermute | solution.py:297
  25.3 0.7 copy-start.5
  25.3 0.9 %copy-start.2 = (bf16[3,384,256]{2,1,0:T(8,128)(2,1)}, bf16[3,384,256]{2,1,0:T(8,128)(2,1)S(1)}, u32[]{:S(2)}) copy-start(bf16[3,384,256]{2,1,0:T(8,128)(2,1)S(1)} %collective-permute-done.4.rest_1_) | copy-start | bytes 1769476
  25.3 1.7 %copy-start = (bf16[768,1536]{1,0:T(8,128)(2,1)}, bf16[768,1536]{1,0:T(8,128)(2,1)S(1)}, u32[]{:S(2)}) copy-start(bf16[768,1536]{1,0:T(8,128)(2,1)S(1)} %collective-permute-done.5.rest_3_) | copy-start | bytes 7077892
